TPU v7x, 128 devices: a whole 4x4x4 slice. The times are simulated.
128 devices in a mesh: samples: 8 (over y, x_hi), space: 16 (over x_lo, z, core).
Axes of the slice: x: 4 (x_hi: 2, x_lo: 2; x = x_hi * 2 + x_lo), y: 4, z: 4, core: 2. Of those that a mesh axis runs over, the one named last changes fastest.
Arguments:
- target: bfloat16 [8, 16384, 8192], P(None, 'samples', 'space'), may hold values from 0 to 1
- a_factor: bfloat16 [16384, 256], P(('samples', 'space')), may hold values from -3 to 3
- b_factor: bfloat16 [8192, 256], P(('space', 'samples')), may hold values from -3 to 3
- c_factor: bfloat16 [8, 256], replicated, may hold values from -3 to 3
Outputs:
- grad_a: float32 [16384, 256], P(('samples', 'space'))
- grad_b: float32 [8192, 256], P(('space', 'samples'))
- grad_c: float32 [8, 256], replicated
All inputs are finite; a program needn't handle non-finite values.
Results may differ from a plain program's by a relative error of at most 0.002.
Values may be sent and summed in bfloat16 or wider, within the bound.
No kernel may reach another device: no remote copies, remote signals or barrier semaphores. Data moves between devices by JAX's collectives and lax.ppermute only.
A program may use at most 128 MiB of HBM per device.

v0:
```python
import jax
import jax.numpy as jnp
from jax import lax
from jax.sharding import PartitionSpec as P


def on_device(target, a_factor, b_factor, c_factor):
    a_full = lax.all_gather(a_factor, "space", axis=0, tiled=True)
    b_full = lax.all_gather(b_factor, "samples", axis=0, tiled=True)
    c_wide = c_factor.astype(jnp.float32)
    scaled = (c_wide[:, None, :] * a_full.astype(jnp.float32)[None]).astype(jnp.bfloat16)
    model = jnp.einsum("kir,jr->kij", scaled, b_full, preferred_element_type=jnp.float32)
    derivative = (jax.nn.sigmoid(model) - target.astype(jnp.float32)).astype(jnp.bfloat16)
    weighted = jnp.einsum("kij,ir->kjr", derivative, a_full, preferred_element_type=jnp.float32)
    b_part = jnp.sum(weighted * c_wide[:, None, :], axis=0)
    c_part = jnp.sum(weighted * b_full.astype(jnp.float32)[None], axis=1)
    own_a = a_factor.shape[0]
    own_b = b_factor.shape[0]
    inner = jnp.einsum("kij,jr->kir", derivative, b_full, preferred_element_type=jnp.float32)
    whole_a = lax.psum(jnp.sum(inner * c_wide[:, None, :], axis=0), "space")
    grad_a = lax.dynamic_slice_in_dim(whole_a, lax.axis_index("space") * own_a, own_a, 0)
    whole_b = lax.psum(b_part, "samples")
    grad_b = lax.dynamic_slice_in_dim(whole_b, lax.axis_index("samples") * own_b, own_b, 0)
    grad_c = lax.psum(c_part, ("samples", "space"))
    return (grad_a, grad_b, grad_c)


def solution(mesh):
    return jax.shard_map(
        on_device,
        mesh=mesh,
        in_specs=(
            P(None, "samples", "space"),
            P(("samples", "space"), None),
            P(("space", "samples"), None),
            P(),
        ),
        out_specs=(P(("samples", "space"), None), P(("space", "samples"), None), P()),
        check_vma=False,
    )
```

profile of v0, /device:TPU:1, one launch (start us, length us, event | category | flops | bytes accessed | tf_op | source)
XLA Modules:
  0.0 294.9 jit_solution(3848630474228114266)
XLA Ops:
  7.2 0.0 all-gather.2.cloned.1.call-start
  7.2 0.7 all-gather.2.cloned.1.call-update
  7.9 0.0 all-reduce.5.cloned.1.call-start
  7.9 0.7 convert_element_type.18
  8.6 30.6 %all_gather.7 = bf16[512,256]{1,0:T(8,128)(2,1)S(1)} all-gather(bf16[64,256]{1,0:T(8,128)(2,1)} %param.6), channel_id=1, replica_groups=mesh['samples'=8,'space'=16] {'samples'}, dimensions={0}, use_global_device_ids=true | all-gather | bytes 294912 | tf_op jit(solution)/shard_map/all_gather | solution.py:9
  39.3 6.7 %all-gather.2.cloned.1.call-done = bf16[2048,256]{1,0:T(8,128)(2,1)} async-done(((bf16[128,256]{1,0:T(8,128)(2,1)}), bf16[2048,256]{1,0:T(8,128)(2,1)}) %all-gather.2.cloned.1.call-update) | async-done | bytes 1048592 | tf_op jit(solution)/shard_map/all_gather | solution.py:8
  46.0 1.4 convert_element_type.19
  47.4 0.0 copy-start
  47.4 17.1 %subtract_convert_fusion = bf16[8,2048,512]{2,1,0:T(8,128)(2,1)} fusion(bf16[8,2048,512]{2,1,0:T(8,128)(2,1)} %param.4, f32[2048,256]{1,0:T(8,128)S(1)} %convert_element_type.19, f32[8,256]{1,0:T(8,128)S(1)} %convert_element_type.18, bf16[512,256]{1,0:T(8,128)(2,1)S(1)} %all_gather.7), kind=kOutput, calls=%fused_computation | convolution fusion | flops 4353687552 | bytes 35921920 | tf_op jit(solution)/shard_map/kir,jr->kij/dot_general | solution.py:12
  64.4 0.0 copy-done
  64.4 11.7 %multiply_reduce_fusion.1 = (f32[8,256]{1,0:T(8,128)S(1)}, f32[512,256]{1,0:T(8,128)}) fusion(f32[512,256]{1,0:T(8,128)S(1)} %convert_element_type.23, f32[8,256]{1,0:T(8,128)S(1)} %convert_element_type.18, bf16[8,2048,512]{2,1,0:T(8,128)(2,1)} %subtract_convert_fusion, bf16[2048,256]{1,0:T(8,128)(2,1)S(1)} %copy-done), kind=kOutput, calls=%fused_computation.5 | convolution fusion | flops 4299028480 | bytes 18890752 | tf_op jit(solution)/shard_map/kij,ir->kjr/dot_general | solution.py:14
  76.2 0.0 all-reduce.5.cloned.1.call-update
  76.2 0.2 all-reduce.3.cloned.1.call-start
  76.4 11.8 %multiply_reduce_fusion = f32[2048,256]{1,0:T(8,128)} fusion(f32[8,256]{1,0:T(8,128)S(1)} %convert_element_type.18, bf16[8,2048,512]{2,1,0:T(8,128)(2,1)} %subtract_convert_fusion, bf16[512,256]{1,0:T(8,128)(2,1)S(1)} %all_gather.7), kind=kOutput, calls=%fused_computation.1 | convolution fusion | flops 4302831616 | bytes 19144704 | tf_op jit(solution)/shard_map/kij,jr->kir/dot_general | solution.py:19
  88.2 0.0 all-reduce.3.cloned.1.call-update
  88.2 66.9 %psum.23 = f32[8,256]{1,0:T(8,128)} all-reduce(f32[8,256]{1,0:T(8,128)S(1)} %get-tuple-element.3), channel_id=1, replica_groups=mesh['samples'=8,'space'=16] {'samples','space'}, use_global_device_ids=true, to_apply=%region_5.0 | all-reduce | flops 2048 | bytes 16384 | tf_op jit(solution)/shard_map/psum | solution.py:24
  155.1 3.3 %all-reduce.5.cloned.1.call-done = f32[512,256]{1,0:T(8,128)} async-done(((f32[512,256]{1,0:T(8,128)}), f32[512,256]{1,0:T(8,128)}) %all-reduce.5.cloned.1.call-update) | async-done | bytes 524304 | tf_op jit(solution)/shard_map/psum | solution.py:22
  158.5 1.5 constant_dynamic-slice_fusion
  160.0 126.8 %all-reduce.3.cloned.1.call-done = f32[2048,256]{1,0:T(8,128)} async-done(((f32[2048,256]{1,0:T(8,128)}), f32[2048,256]{1,0:T(8,128)}) %all-reduce.3.cloned.1.call-update) | async-done | bytes 2097168 | tf_op jit(solution)/shard_map/psum | solution.py:20
  286.8 1.6 constant_dynamic-slice_fusion.1
  (1 shorter events, 0.0 us)
Async XLA Ops:
  7.2 38.8 %all-gather.2.cloned.1.call-start = ((), (), s32[]{:S(2)}) async-start(), calls=%async_computation | async-start | bytes 1114112 | tf_op jit(solution)/shard_map/all_gather | solution.py:8
  7.9 150.6 %all-reduce.5.cloned.1.call-start = ((), (), s32[]{:S(2)}) async-start(), calls=%async_computation.2 | async-start | bytes 1048576 | tf_op jit(solution)/shard_map/psum | solution.py:22
  47.4 17.1 %copy-start = (bf16[2048,256]{1,0:T(8,128)(2,1)S(1)}, bf16[2048,256]{1,0:T(8,128)(2,1)}, u32[]{:S(2)}) copy-start(bf16[2048,256]{1,0:T(8,128)(2,1)} %all-gather.2.cloned.1.call-done) | copy-start | bytes 3145732
  76.2 210.6 %all-reduce.3.cloned.1.call-start = ((), (), s32[]{:S(2)}) async-start(), calls=%async_computation.1 | async-start | bytes 4194304 | tf_op jit(solution)/shard_map/psum | solution.py:20
Sparse Core Ops, SparseCore 0:
  9.7 36.2 all-gather.1
  76.3 82.1 all-reduce.4
  161.1 125.5 all-reduce.2
where the time goes:
time: 295 us
  waiting for transfers between devices  138 us (47%)
  blocking collectives  97.5 us (33%)
  matrix products  40.6 us (14%)
  between operations  13.8 us (5%)
  local copies, waits for them, and re-layouts  3.04 us (1%)
    psum x1, waiting for transfers between devices, on_device(): whole_a = lax.psum(jnp.sum(inner * c_wide[:, None, :], axis=0), 'space')  127 us
    psum x1, blocking collectives, on_device(): grad_c = lax.psum(c_part, ('samples', 'space'))  66.9 us
    all_gather x1, blocking collectives, on_device(): b_full = lax.all_gather(b_factor, 'samples', axis=0, tiled=True)  30.6 us
    dot_general x1, matrix products, on_device(): jnp.einsum('kir,jr->kij', scaled, b_full, preferred_element_type=jnp.floa...  17.1 us
    dot_general x1, matrix products, on_device(): jnp.einsum('kij,jr->kir', derivative, b_full, preferred_element_type=jnp....  11.8 us
    dot_general x1, matrix products, on_device(): jnp.einsum('kij,ir->kjr', derivative, a_full, preferred_element_type=jnp....  11.7 us
    all_gather x1, waiting for transfers between devices, on_device(): a_full = lax.all_gather(a_factor, 'space', axis=0, tiled=True)  6.71 us
  transfers between devices with their start and end apart: 3, of which 3 were waited for; matrix products, arithmetic and copies ran while one was open for 5% of the time, Pallas kernels for 0%

commit v1 on v0

--- a/solution.py
+++ b/solution.py
@@ -6,7 +6,8 @@
 
 def on_device(target, a_factor, b_factor, c_factor):
     a_full = lax.all_gather(a_factor, "space", axis=0, tiled=True)
-    b_full = lax.all_gather(b_factor, "samples", axis=0, tiled=True)
+    sent = jnp.stack([b_factor] * lax.axis_size("samples"))
+    b_full = jnp.concatenate(lax.all_to_all(sent, "samples", 0, 0), axis=0)
     c_wide = c_factor.astype(jnp.float32)
     scaled = (c_wide[:, None, :] * a_full.astype(jnp.float32)[None]).astype(jnp.bfloat16)
     model = jnp.einsum("kir,jr->kij", scaled, b_full, preferred_element_type=jnp.float32)

time: 295 us -> 294 us (level)
  blocking collectives: 97.5 us -> 66.7 us
  waiting for transfers between devices: 138 us -> 158 us
  starting transfers between devices: 0.3 us -> 7.78 us
    all_gather x1 -> x0, blocking collectives: 30.6 us -> none  [on_device(): b_full = lax.all_gather(b_factor, 'samples', axis=0, tiled=True)]
    all_gather x1, waiting for transfers between devices: 6.71 us -> 21.4 us  [on_device(): a_full = lax.all_gather(a_factor, 'space', axis=0, tiled=True)]
    all_to_all x0 -> x1, starting transfers between devices: none -> 7.48 us  [on_device(): b_full = jnp.concatenate(lax.all_to_all(sent, 'samples', 0, 0), axis=0)]
    all_to_all x0 -> x1, waiting for transfers between devices: none -> 6.9 us  [on_device(): b_full = jnp.concatenate(lax.all_to_all(sent, 'samples', 0, 0), axis=0)]
  transfers between devices with their start and end apart: 3 -> 4, of which waited for: 3 -> 4; matrix products, arithmetic and copies ran while one was open for 5% -> 5% of each run, Pallas kernels for 0% -> 0%
where the time goes in v1:
time: 294 us; the launch traced here: 293 us
  waiting for transfers between devices  158 us (54%)
  blocking collectives  66.7 us (23%)
  matrix products  40.6 us (14%)
  between operations  13.8 us (5%)
  starting transfers between devices  7.78 us (3%)
  local copies, waits for them, and re-layouts  4.51 us (2%)
    psum x1, waiting for transfers between devices, on_device(): whole_a = lax.psum(jnp.sum(inner * c_wide[:, None, :], axis=0), 'space')  127 us
    psum x1, blocking collectives, on_device(): grad_c = lax.psum(c_part, ('samples', 'space'))  66.7 us
    all_gather x1, waiting for transfers between devices, on_device(): a_full = lax.all_gather(a_factor, 'space', axis=0, tiled=True)  21.4 us
    dot_general x1, matrix products, on_device(): jnp.einsum('kir,jr->kij', scaled, b_full, preferred_element_type=jnp.floa...  17.1 us
    dot_general x1, matrix products, on_device(): jnp.einsum('kij,jr->kir', derivative, b_full, preferred_element_type=jnp....  11.8 us
    dot_general x1, matrix products, on_device(): jnp.einsum('kij,ir->kjr', derivative, a_full, preferred_element_type=jnp....  11.7 us
    all_to_all x1, starting transfers between devices, on_device(): b_full = jnp.concatenate(lax.all_to_all(sent, 'samples', 0, 0), axis=0)  7.48 us
    all_to_all x1, waiting for transfers between devices, on_device(): b_full = jnp.concatenate(lax.all_to_all(sent, 'samples', 0, 0), axis=0)  6.9 us
  transfers between devices with their start and end apart: 4, of which 4 were waited for; matrix products, arithmetic and copies ran while one was open for 5% of the time, Pallas kernels for 0%

profile of v1, /device:TPU:1, one launch (start us, length us, event | category | flops | bytes accessed | tf_op | source)
XLA Modules:
  0.0 293.2 jit_solution(5684274755794992528)
XLA Ops:
  7.2 0.0 all-gather.2.cloned.1.call-start
  7.2 0.7 all-gather.2.cloned.1.call-update
  7.9 1.5 stack.2
  9.4 7.5 %all-to-all-start = ((bf16[8,64,256]{2,1,0:T(8,128)(2,1)}), bf16[8,64,256]{2,1,0:T(8,128)(2,1)S(1)}, u32[]{:S(2)}, u32[]{:S(2)}) async-start(bf16[8,64,256]{2,1,0:T(8,128)(2,1)} %stack.2), calls=%async_computation | async-start | bytes 524288 | tf_op jit(solution)/shard_map/all_to_all | solution.py:10
  16.8 0.0 all-reduce.5.cloned.1.call-start
  16.9 0.7 convert_element_type.22
  17.6 6.9 %all-to-all-done = bf16[8,64,256]{2,1,0:T(8,128)(2,1)S(1)} async-done(((bf16[8,64,256]{2,1,0:T(8,128)(2,1)}), bf16[8,64,256]{2,1,0:T(8,128)(2,1)S(1)}, u32[]{:S(2)}, u32[]{:S(2)}) %all-to-all-start) | async-done | bytes 262176 | tf_op jit(solution)/shard_map/all_to_all | solution.py:10
  24.5 0.1 bitcast_convert_fusion
  24.5 21.4 %all-gather.2.cloned.1.call-done = bf16[2048,256]{1,0:T(8,128)(2,1)} async-done(((bf16[128,256]{1,0:T(8,128)(2,1)}), bf16[2048,256]{1,0:T(8,128)(2,1)}) %all-gather.2.cloned.1.call-update) | async-done | bytes 1048592 | tf_op jit(solution)/shard_map/all_gather | solution.py:8
  45.9 1.4 convert_element_type.23
  47.3 0.0 copy-start
  47.3 17.1 %subtract_convert_fusion = bf16[8,2048,512]{2,1,0:T(8,128)(2,1)} fusion(bf16[8,2048,512]{2,1,0:T(8,128)(2,1)} %param.4, bf16[512,256,1]{1,0,2:T(8,128)(2,1)S(1)} %bitcast.13, f32[2048,256]{1,0:T(8,128)S(1)} %convert_element_type.23, f32[8,256]{1,0:T(8,128)S(1)} %convert_element_type.22), kind=kOutput, calls=%fused_computation | convolution fusion | flops 4353687552 | bytes 35921920 | tf_op jit(solution)/shard_map/kir,jr->kij/dot_general | solution.py:13
  64.4 0.0 copy-done
  64.4 11.7 %multiply_reduce_fusion.1 = (f32[8,256]{1,0:T(8,128)S(1)}, f32[512,256]{1,0:T(8,128)}) fusion(f32[512,256]{1,0:T(8,128)S(1)} %bitcast_convert_fusion, f32[8,256]{1,0:T(8,128)S(1)} %convert_element_type.22, bf16[8,2048,512]{2,1,0:T(8,128)(2,1)} %subtract_convert_fusion, bf16[2048,256]{1,0:T(8,128)(2,1)S(1)} %copy-done), kind=kOutput, calls=%fused_computation.5 | convolution fusion | flops 4299028480 | bytes 18890752 | tf_op jit(solution)/shard_map/kij,ir->kjr/dot_general | solution.py:15
  76.1 0.0 all-reduce.5.cloned.1.call-update
  76.1 0.2 all-reduce.3.cloned.1.call-start
  76.4 11.8 %multiply_reduce_fusion = f32[2048,256]{1,0:T(8,128)} fusion(f32[8,256]{1,0:T(8,128)S(1)} %convert_element_type.22, bf16[8,2048,512]{2,1,0:T(8,128)(2,1)} %subtract_convert_fusion, bf16[512,256,1]{1,0,2:T(8,128)(2,1)S(1)} %bitcast.14), kind=kOutput, calls=%fused_computation.1 | convolution fusion | flops 4302831616 | bytes 19144704 | tf_op jit(solution)/shard_map/kij,jr->kir/dot_general | solution.py:20
  88.2 0.0 all-reduce.3.cloned.1.call-update
  88.2 66.7 %psum.23 = f32[8,256]{1,0:T(8,128)} all-reduce(f32[8,256]{1,0:T(8,128)S(1)} %get-tuple-element.3), channel_id=1, replica_groups=mesh['samples'=8,'space'=16] {'samples','space'}, use_global_device_ids=true, to_apply=%region_5.0 | all-reduce | flops 2048 | bytes 16384 | tf_op jit(solution)/shard_map/psum | solution.py:25
  154.9 2.0 all-reduce.5.cloned.1.call-done
  156.9 1.5 constant_dynamic-slice_fusion
  158.4 126.7 %all-reduce.3.cloned.1.call-done = f32[2048,256]{1,0:T(8,128)} async-done(((f32[2048,256]{1,0:T(8,128)}), f32[2048,256]{1,0:T(8,128)}) %all-reduce.3.cloned.1.call-update) | async-done | bytes 2097168 | tf_op jit(solution)/shard_map/psum | solution.py:21
  285.1 1.6 constant_dynamic-slice_fusion.1
Async XLA Ops:
  7.2 38.8 %all-gather.2.cloned.1.call-start = ((), (), s32[]{:S(2)}) async-start(), calls=%async_computation.1 | async-start | bytes 1114112 | tf_op jit(solution)/shard_map/all_gather | solution.py:8
  9.4 15.1 %all-to-all-start = ((bf16[8,64,256]{2,1,0:T(8,128)(2,1)}), bf16[8,64,256]{2,1,0:T(8,128)(2,1)S(1)}, u32[]{:S(2)}, u32[]{:S(2)}) async-start(bf16[8,64,256]{2,1,0:T(8,128)(2,1)} %stack.2), calls=%async_computation | async-start | bytes 524288 | tf_op jit(solution)/shard_map/all_to_all | solution.py:10
  16.8 140.1 %all-reduce.5.cloned.1.call-start = ((), (), s32[]{:S(2)}) async-start(), calls=%async_computation.3 | async-start | bytes 1048576 | tf_op jit(solution)/shard_map/psum | solution.py:23
  47.3 17.1 %copy-start = (bf16[2048,256]{1,0:T(8,128)(2,1)S(1)}, bf16[2048,256]{1,0:T(8,128)(2,1)}, u32[]{:S(2)}) copy-start(bf16[2048,256]{1,0:T(8,128)(2,1)} %all-gather.2.cloned.1.call-done) | copy-start | bytes 3145732
  76.1 209.0 %all-reduce.3.cloned.1.call-start = ((), (), s32[]{:S(2)}) async-start(), calls=%async_computation.2 | async-start | bytes 4194304 | tf_op jit(solution)/shard_map/psum | solution.py:21
Sparse Core Ops, SparseCore 0:
  9.7 36.1 all-gather.1
  76.3 80.6 all-reduce.4
  159.6 125.4 all-reduce.2

commit v2 on v0

--- a/solution.py
+++ b/solution.py
@@ -17,7 +17,9 @@
     own_a = a_factor.shape[0]
     own_b = b_factor.shape[0]
     inner = jnp.einsum("kij,jr->kir", derivative, b_full, preferred_element_type=jnp.float32)
-    whole_a = lax.psum(jnp.sum(inner * c_wide[:, None, :], axis=0), "space")
+    own = jnp.sum(inner * c_wide[:, None, :], axis=0)
+    parts = lax.all_gather(own, "space", axis=0, tiled=False)
+    whole_a = parts.sum(axis=0)
     grad_a = lax.dynamic_slice_in_dim(whole_a, lax.axis_index("space") * own_a, own_a, 0)
     whole_b = lax.psum(b_part, "samples")
     grad_b = lax.dynamic_slice_in_dim(whole_b, lax.axis_index("samples") * own_b, own_b, 0)

time: 295 us -> 354 us (1.20)
  waiting for transfers between devices: 138 us -> 185 us
  other arithmetic: 2.11 us -> 14.2 us
    all_gather x0 -> x1, waiting for transfers between devices: none -> 174 us  [on_device(): parts = lax.all_gather(own, 'space', axis=0, tiled=False)]
    psum x1 -> x0, waiting for transfers between devices: 127 us -> none  [on_device(): whole_a = lax.psum(jnp.sum(inner * c_wide[:, None, :], axis=0), 'space')]
    reduce_sum x0 -> x1, other arithmetic: none -> 12.1 us  [on_device(): whole_a = parts.sum(axis=0)]
  transfers between devices with their start and end apart: 3 -> 3, of which waited for: 3 -> 3; matrix products, arithmetic and copies ran while one was open for 5% -> 4% of each run, Pallas kernels for 0% -> 0%
where the time goes in v2:
time: 354 us; the launch traced here: 353 us
  waiting for transfers between devices  185 us (52%)
  blocking collectives  97.5 us (28%)
  matrix products  40.5 us (11%)
  other arithmetic  14.2 us (4%)
  between operations  13.8 us (4%)
    all_gather x1, waiting for transfers between devices, on_device(): parts = lax.all_gather(own, 'space', axis=0, tiled=False)  174 us
    psum x1, blocking collectives, on_device(): grad_c = lax.psum(c_part, ('samples', 'space'))  66.9 us
    all_gather x1, blocking collectives, on_device(): b_full = lax.all_gather(b_factor, 'samples', axis=0, tiled=True)  30.6 us
    dot_general x1, matrix products, on_device(): jnp.einsum('kir,jr->kij', scaled, b_full, preferred_element_type=jnp.floa...  17.1 us
    reduce_sum x1, other arithmetic, on_device(): whole_a = parts.sum(axis=0)  12.1 us
    dot_general x1, matrix products, on_device(): jnp.einsum('kij,jr->kir', derivative, b_full, preferred_element_type=jnp....  11.8 us
    dot_general x1, matrix products, on_device(): jnp.einsum('kij,ir->kjr', derivative, a_full, preferred_element_type=jnp....  11.7 us
  transfers between devices with their start and end apart: 3, of which 3 were waited for; matrix products, arithmetic and copies ran while one was open for 4% of the time, Pallas kernels for 0%

profile of v2, /device:TPU:1, one launch (start us, length us, event | category | flops | bytes accessed | tf_op | source)
XLA Modules:
  0.0 353.4 jit_solution(2482330960223403645)
XLA Ops:
  7.2 0.0 all-gather.4.cloned.1.call-start
  7.2 0.7 all-gather.4.cloned.1.call-update
  7.9 0.0 all-reduce.2.cloned.1.call-start
  7.9 0.7 convert_element_type.18
  8.6 30.6 %all_gather.13 = bf16[512,256]{1,0:T(8,128)(2,1)S(1)} all-gather(bf16[64,256]{1,0:T(8,128)(2,1)} %param.6), channel_id=1, replica_groups=mesh['samples'=8,'space'=16] {'samples'}, dimensions={0}, use_global_device_ids=true | all-gather | bytes 294912 | tf_op jit(solution)/shard_map/all_gather | solution.py:9
  39.3 6.7 %all-gather.4.cloned.1.call-done = bf16[2048,256]{1,0:T(8,128)(2,1)} async-done(((bf16[128,256]{1,0:T(8,128)(2,1)}), bf16[2048,256]{1,0:T(8,128)(2,1)}) %all-gather.4.cloned.1.call-update) | async-done | bytes 1048592 | tf_op jit(solution)/shard_map/all_gather | solution.py:8
  46.0 1.4 convert_element_type.19
  47.4 0.0 copy-start
  47.4 17.1 %subtract_convert_fusion = bf16[8,2048,512]{2,1,0:T(8,128)(2,1)} fusion(bf16[8,2048,512]{2,1,0:T(8,128)(2,1)} %param.4, f32[2048,256]{1,0:T(8,128)S(1)} %convert_element_type.19, f32[8,256]{1,0:T(8,128)S(1)} %convert_element_type.18, bf16[512,256]{1,0:T(8,128)(2,1)S(1)} %all_gather.13), kind=kOutput, calls=%fused_computation | convolution fusion | flops 4353687552 | bytes 35921920 | tf_op jit(solution)/shard_map/kir,jr->kij/dot_general | solution.py:12
  64.4 0.0 copy-done
  64.4 11.7 %multiply_reduce_fusion.1 = (f32[8,256]{1,0:T(8,128)S(1)}, f32[512,256]{1,0:T(8,128)}) fusion(f32[512,256]{1,0:T(8,128)S(1)} %convert_element_type.23, f32[8,256]{1,0:T(8,128)S(1)} %convert_element_type.18, bf16[8,2048,512]{2,1,0:T(8,128)(2,1)} %subtract_convert_fusion, bf16[2048,256]{1,0:T(8,128)(2,1)S(1)} %copy-done), kind=kOutput, calls=%fused_computation.5 | convolution fusion | flops 4299028480 | bytes 18890752 | tf_op jit(solution)/shard_map/kij,ir->kjr/dot_general | solution.py:14
  76.1 0.0 all-reduce.2.cloned.1.call-update
  76.2 0.2 all-gather.6.cloned.1.call-start
  76.4 11.8 %multiply_reduce_fusion = f32[2048,256]{1,0:T(8,128)} fusion(f32[8,256]{1,0:T(8,128)S(1)} %convert_element_type.18, bf16[8,2048,512]{2,1,0:T(8,128)(2,1)} %subtract_convert_fusion, bf16[512,256]{1,0:T(8,128)(2,1)S(1)} %all_gather.13), kind=kOutput, calls=%fused_computation.1 | convolution fusion | flops 4302831616 | bytes 19144704 | tf_op jit(solution)/shard_map/kij,jr->kir/dot_general | solution.py:19
  88.2 0.0 all-gather.6.cloned.1.call-update
  88.2 66.9 %psum.15 = f32[8,256]{1,0:T(8,128)} all-reduce(f32[8,256]{1,0:T(8,128)S(1)} %get-tuple-element.3), channel_id=1, replica_groups=mesh['samples'=8,'space'=16] {'samples','space'}, use_global_device_ids=true, to_apply=%region_5.0 | all-reduce | flops 2048 | bytes 16384 | tf_op jit(solution)/shard_map/psum | solution.py:26
  155.1 3.3 all-reduce.2.cloned.1.call-done
  158.4 1.5 constant_dynamic-slice_fusion
  159.9 174.2 %all-gather.6.cloned.1.call-done = f32[32768,256]{1,0:T(8,128)} async-done(((f32[2048,256]{1,0:T(8,128)}), f32[32768,256]{1,0:T(8,128)}) %all-gather.6.cloned.1.call-update) | async-done | bytes 33554448 | tf_op jit(solution)/shard_map/all_gather | solution.py:21
  334.1 12.1 %reduce_sum.37 = f32[2048,256]{1,0:T(8,128)S(1)} reduce(f32[16,2048,256]{2,1,0:T(8,128)} %bitcast.13, f32[]{:T(128)} %constant.4.clone.1), dimensions={0}, to_apply=%region_1.0 | reduce | flops 7864320 | bytes 35651588 | tf_op jit(solution)/shard_map/reduce_sum | solution.py:22
  346.2 0.7 constant_dynamic-slice_fusion.1
  (1 shorter events, 0.0 us)
Async XLA Ops:
  7.2 38.8 %all-gather.4.cloned.1.call-start = ((), (), s32[]{:S(2)}) async-start(), calls=%async_computation | async-start | bytes 1114112 | tf_op jit(solution)/shard_map/all_gather | solution.py:8
  7.9 150.5 %all-reduce.2.cloned.1.call-start = ((), (), s32[]{:S(2)}) async-start(), calls=%async_computation.1 | async-start | bytes 1048576 | tf_op jit(solution)/shard_map/psum | solution.py:24
  47.4 17.1 %copy-start = (bf16[2048,256]{1,0:T(8,128)(2,1)S(1)}, bf16[2048,256]{1,0:T(8,128)(2,1)}, u32[]{:S(2)}) copy-start(bf16[2048,256]{1,0:T(8,128)(2,1)} %all-gather.4.cloned.1.call-done) | copy-start | bytes 3145732
  76.2 257.9 %all-gather.6.cloned.1.call-start = ((), (), s32[]{:S(2)}) async-start(), calls=%async_computation.2 | async-start | bytes 35651584 | tf_op jit(solution)/shard_map/all_gather | solution.py:21
Sparse Core Ops, SparseCore 0:
  9.7 36.2 all-gather.3
  76.3 82.1 all-reduce.1
  160.3 173.7 all-gather.5
